TPU v7x, 128 devices: a whole 4x4x4 slice. The times are simulated.
128 devices in a mesh: row: 16 (over z, y), col: 8 (over x, core).
Axes of the slice: x: 4, y: 4, z: 4, core: 2. Of those that a mesh axis runs over, the one named last changes fastest.
Arguments:
- trailing: float32 [16384, 16384], P('row', 'col'), may hold values from -40 to 40, as said below
- factor_one: float32 [16384, 512], P(('row', 'col')), may hold values from -0.0390625 to 0.0390625
- inverse_one: float32 [512, 512], replicated, may hold values from -1 to 2, as said below
- factor_two_top: float32 [512, 512], replicated, may hold values from -0.0390625 to 0.0390625
- factor_two: float32 [16384, 512], P(('row', 'col')), may hold values from -0.0390625 to 0.0390625
- inverse_two: float32 [512, 512], replicated, may hold values from -1 to 2, as said below
- structure_one: int32 [96], replicated, may hold values from 0 to 127, as said below
- structure_two: int32 [94], replicated, may hold values from 0 to 127, as said below
Outputs:
- column_one: float32 [16384, 512], P(('row', 'col'))
- diagonal_one: float32 [512, 512], replicated
- column_two: float32 [16384, 512], P(('row', 'col'))
- cross_two: float32 [512, 512], replicated
- diagonal_two: float32 [512, 512], replicated
Inputs may be any that keep to these rules, and one draw needn't show every extreme that they name: `trailing`: symmetric. `inverse_one`: lower triangular, diagonal between 1 and 2. `inverse_two`: lower triangular, diagonal between 1 and 2. `structure_one`: distinct, rising; lists block 0 and the last block. `structure_two`: distinct, rising, each also listed in structure_one; lists block 0 and the last block.
All inputs are finite; a program needn't handle non-finite values.
Results may differ from a plain program's by a relative error of at most 0.0003.
Values sent between devices are 32-bit elements; how exact they have to be, the bound alone decides.
No kernel may reach another device: no remote copies, remote signals or barrier semaphores. Data moves between devices by JAX's collectives and lax.ppermute only.
A program may use at most 128 MiB of HBM per device.

v0:
```python
import jax
import jax.numpy as jnp
from jax import lax
from jax.sharding import PartitionSpec as P

BLK = 128


def spread(x, axis, root):
    mine = lax.axis_index(axis) == root
    return lax.psum(jnp.where(mine, x, jnp.zeros_like(x)), axis)


def product(left, right):
    return jnp.dot(left, right, precision=lax.Precision.HIGHEST, preferred_element_type=jnp.float32)


def block_flags(structure, first_row, count):
    blocks = (first_row + jnp.arange(count, dtype=jnp.int32)) // BLK
    hits = jnp.any(blocks[:, None] == structure[None, :], axis=1)
    return hits.astype(jnp.float32)[:, None]


def panel_apart(normal, col_index, spread_count):
    row_block = lax.all_gather(normal, "col", axis=0, tiled=True)
    pieces = []
    for offset in range(spread_count):
        pieces.append(spread(row_block, "row", col_index * spread_count + offset))
    return (row_block, jnp.concatenate(pieces, axis=0))


def sweep(trailing, col_block, own_normal):
    summed = lax.psum_scatter(-product(trailing, col_block), "col", scatter_dimension=0, tiled=True)
    quad_part = product(own_normal.T, summed)
    return (summed, quad_part)


def body(
    trailing,
    factor_one,
    inverse_one,
    factor_two_top,
    factor_two,
    inverse_two,
    structure_one,
    structure_two,
):
    piece_rows = factor_one.shape[0]
    spread_count = lax.axis_size("row") // lax.axis_size("col")
    row_index = lax.axis_index("row")
    col_index = lax.axis_index("col")
    first_row = (row_index * lax.axis_size("col") + col_index) * piece_rows
    mask_one = block_flags(structure_one, first_row, piece_rows)
    mask_two = block_flags(structure_two, first_row, piece_rows)
    normal_one = mask_one * product(factor_one, inverse_one)
    normal_two = mask_two * product(factor_two, inverse_two)
    rows_one, cols_one = panel_apart(normal_one, col_index, spread_count)
    rows_two, cols_two = panel_apart(normal_two, col_index, spread_count)
    summed_one, quad_one = sweep(trailing, cols_one, normal_one)
    column_one = mask_one * summed_one
    diag_total = lax.psum(quad_one, ("row", "col"))
    diagonal_one = product(inverse_one.T, inverse_one) - diag_total
    normal_top = product(factor_two_top, inverse_two)
    summed_two, quad_two = sweep(trailing, cols_two, normal_two)
    local_part = -product(column_one, normal_top)
    column_two = mask_two * (local_part + summed_two)
    cross_total, second_total = lax.psum(
        (product(column_one.T, normal_two), product(normal_two.T, local_part) + quad_two),
        ("row", "col"),
    )
    cross_two = -(product(diagonal_one, normal_top) + cross_total)
    diagonal_two = (
        product(inverse_two.T, inverse_two) - product(normal_top.T, cross_two) - second_total
    )
    return (column_one, diagonal_one, column_two, cross_two, diagonal_two)


def solution(mesh):
    return jax.shard_map(
        body,
        mesh=mesh,
        in_specs=(
            P("row", "col"),
            P(("row", "col"), None),
            P(),
            P(),
            P(("row", "col"), None),
            P(),
            P(),
            P(),
        ),
        out_specs=(P(("row", "col"), None), P(), P(("row", "col"), None), P(), P()),
        check_vma=False,
    )
```

profile of v0, /device:TPU:1, one launch (start us, length us, event | category | flops | bytes accessed | tf_op | source)
XLA Modules:
  0.0 474.7 jit_solution(2318638378639296707)
XLA Ops:
  7.3 0.9 compare_reduce_fusion
  8.4 2.4 convolution_multiply_fusion
  11.6 2.4 convolution_multiply_fusion.1
  14.1 25.6 %all-gather.5.cloned.1.call-done = f32[1024,512]{1,0:T(8,128)} async-done(((f32[128,512]{1,0:T(8,128)}), f32[1024,512]{1,0:T(8,128)}) %all-gather.5.cloned.1.call-update) | async-done | bytes 2097168 | tf_op jit(solution)/shard_map/all_gather | solution.py:25
  39.7 4.2 broadcast_select_fusion.1
  43.9 23.5 %all-gather.3.cloned.1.call-done = f32[1024,512]{1,0:T(8,128)} async-done(((f32[128,512]{1,0:T(8,128)}), f32[1024,512]{1,0:T(8,128)}) %all-gather.3.cloned.1.call-update) | async-done | bytes 2097168 | tf_op jit(solution)/shard_map/all_gather | solution.py:25
  67.5 4.2 broadcast_select_fusion.3
  71.7 142.3 %all-reduce.7.cloned.1.call-done = (f32[1024,512]{1,0:T(8,128)}, f32[1024,512]{1,0:T(8,128)}, f32[1024,512]{1,0:T(8,128)}, f32[1024,512]{1,0:T(8,128)}) async-done(((f32[1024,512]{1,0:T(8,128)}, f32[1024,512]{1,0:T(8,128)}, f32[1024,512]{1,0:T(8,128)}, f32[1024,512]{1,0:T(8,128)}), (f32[1024,512]{1,0:T(8,128)}, f32[1024,512]{1,0:T(8,128)}, f32[1024,512]{1,0:T(8,128)}, ...) | async-done | bytes 8388624 | tf_op jit(solution)/shard_map/psum | solution.py:11
  214.0 17.6 %negate_bitcast_fusion.1 = f32[1024,512]{1,0:T(8,128)} fusion(f32[1024,2048]{1,0:T(8,128)} %param.8, f32[1024,512]{1,0:T(8,128)} %get-tuple-element.8, f32[1024,512]{1,0:T(8,128)} %get-tuple-element.9), kind=kOutput, calls=%fused_computation.9 | convolution fusion | flops 12886474752 | bytes 14680064 | tf_op jit(solution)/shard_map/dot_general | solution.py:15
  231.8 17.7 %negate_bitcast_fusion = f32[1024,512]{1,0:T(8,128)} fusion(f32[1024,2048]{1,0:T(8,128)} %param.8, f32[1024,512]{1,0:T(8,128)} %get-tuple-element.10, f32[1024,512]{1,0:T(8,128)} %get-tuple-element.11), kind=kOutput, calls=%fused_computation.8 | convolution fusion | flops 12886474752 | bytes 14680064 | tf_op jit(solution)/shard_map/dot_general | solution.py:15
  249.7 3.1 fusion.17
  252.8 9.0 %reduce-scatter.3.cloned.1.call-done = f32[128,512]{1,0:T(8,128)} async-done(((f32[1024,512]{1,0:T(8,128)}), f32[128,512]{1,0:T(8,128)}) %reduce-scatter.3.cloned.1.call-update) | async-done | bytes 262160 | tf_op jit(solution)/shard_map/reduce_scatter | solution.py:33
  261.8 1.0 broadcast_multiply_fusion
  263.6 2.0 fusion.18
  265.6 31.1 %reduce-scatter.5.cloned.1.call-done = f32[128,512]{1,0:T(8,128)} async-done(((f32[1024,512]{1,0:T(8,128)}), f32[128,512]{1,0:T(8,128)}) %reduce-scatter.5.cloned.1.call-update) | async-done | bytes 262160 | tf_op jit(solution)/shard_map/reduce_scatter | solution.py:33
  296.7 2.5 add_multiply_fusion
  299.2 1.0 fusion.20
  300.3 2.0 fusion.16
  302.3 2.0 convolution_add_fusion.1
  304.3 2.9 fusion.19
  307.2 152.7 %all-reduce.5.cloned.1.call-done = (f32[512,512]{1,0:T(8,128)}, f32[512,512]{1,0:T(8,128)}, f32[512,512]{1,0:T(8,128)}) async-done(((f32[512,512]{1,0:T(8,128)}, f32[512,512]{1,0:T(8,128)}, f32[512,512]{1,0:T(8,128)}), (f32[512,512]{1,0:T(8,128)}, f32[512,512]{1,0:T(8,128)}, f32[512,512]{1,0:T(8,128)})) %all-reduce.5.cloned.1.call-update) | async-done | bytes 3145744 | tf_op jit(solution)/shard_map/psum | solution.py:61
  459.8 3.2 convolution_subtract_fusion.1
  463.1 1.9 fusion.13
  465.0 2.9 fusion.12
  (40 shorter events, 2.3 us)
Async XLA Ops:
  7.2 1.2 copy-start
  7.2 4.4 copy-start.1
  7.2 32.5 %all-gather.5.cloned.1.call-start = ((), (), s32[]{:S(2)}) async-start(), calls=%async_computation.4 | async-start | bytes 2359296 | tf_op jit(solution)/shard_map/all_gather | solution.py:25
  10.8 56.7 %all-gather.3.cloned.1.call-start = ((), (), s32[]{:S(2)}) async-start(), calls=%async_computation.2 | async-start | bytes 2359296 | tf_op jit(solution)/shard_map/all_gather | solution.py:25
  14.0 200.0 %all-reduce.7.cloned.1.call-start = ((), (), s32[]{:S(2)}) async-start(), calls=%async_computation.7 | async-start | bytes 16777216 | tf_op jit(solution)/shard_map/psum | solution.py:11
  71.7 190.2 %reduce-scatter.3.cloned.1.call-start = ((), (), s32[]{:S(2)}) async-start(), calls=%async_computation.3 | async-start | bytes 2359296 | tf_op jit(solution)/shard_map/reduce_scatter | solution.py:33
  231.7 65.0 %reduce-scatter.5.cloned.1.call-start = ((), (), s32[]{:S(2)}) async-start(), calls=%async_computation.5 | async-start | bytes 2359296 | tf_op jit(solution)/shard_map/reduce_scatter | solution.py:33
  249.5 14.1 %copy-start.2 = (f32[128,512]{1,0:T(8,128)S(1)}, f32[128,512]{1,0:T(8,128)}, u32[]{:S(2)}) copy-start(f32[128,512]{1,0:T(8,128)} %convolution_multiply_fusion) | copy-start | bytes 786436
  249.5 210.4 %all-reduce.5.cloned.1.call-start = ((), (), s32[]{:S(2)}) async-start(), calls=%async_computation.6 | async-start | bytes 6291456 | tf_op jit(solution)/shard_map/psum | solution.py:61
  262.9 0.7 copy-start.6
  296.7 3.6 copy-start.7
  296.7 3.6 copy-start.10
  299.2 3.1 copy-start.9
  459.8 3.2 copy-start.11
  463.0 1.9 copy-start.5
  463.0 1.9 copy-start.3
  463.1 1.9 copy-start.8
  464.9 2.9 copy-start.4
Sparse Core Ops, SparseCore 0:
  10.9 28.7 all-gather.4
  42.0 25.4 all-gather.2
  71.8 142.2 all-reduce.6
  231.8 29.9 reduce-scatter.2
  264.2 32.4 reduce-scatter.4
  304.5 155.3 all-reduce.4
where the time goes:
time: 475 us
  waiting for transfers between devices  384 us (81%)
  matrix products  63.5 us (13%)
  between operations  14.3 us (3%)
  other arithmetic  11.1 us (2%)
    psum x1, waiting for transfers between devices, body(): diag_total = lax.psum(quad_one, ('row', 'col'))  153 us
    psum x1, waiting for transfers between devices, spread(): return lax.psum(jnp.where(mine, x, jnp.zeros_like(x)), axis)  142 us
    dot_general x14, matrix products, product(): jnp.dot(left, right, precision=lax.Precision.HIGHEST, preferred_element_t...  63.5 us
    all_gather x2, waiting for transfers between devices, panel_apart(): row_block = lax.all_gather(normal, 'col', axis=0, tiled=True)  49.2 us
    reduce_scatter x2, waiting for transfers between devices, sweep(): lax.psum_scatter(-product(trailing, col_block), 'col', scatter_dimension=...  40.2 us
  transfers between devices with their start and end apart: 6, of which 6 were waited for; matrix products, arithmetic and copies ran while one was open for 7% of the time, Pallas kernels for 0%

commit v1 on v0

--- a/solution.py
+++ b/solution.py
@@ -58,7 +58,8 @@
     rows_two, cols_two = panel_apart(normal_two, col_index, spread_count)
     summed_one, quad_one = sweep(trailing, cols_one, normal_one)
     column_one = mask_one * summed_one
-    diag_total = lax.psum(quad_one, ("row", "col"))
+    half = lax.psum(quad_one, "col")
+    diag_total = lax.psum(half, "row")
     diagonal_one = product(inverse_one.T, inverse_one) - diag_total
     normal_top = product(factor_two_top, inverse_two)
     summed_two, quad_two = sweep(trailing, cols_two, normal_two)

time: 475 us -> 627 us (1.32)
  waiting for transfers between devices: 384 us -> 538 us
    psum x1 -> x3, waiting for transfers between devices: 153 us -> 326 us  [the longest x1 149 us: body(): lax.psum((product(column_one.T, normal_two), product(normal_two.T, local_...]
    psum x1, waiting for transfers between devices: 142 us -> 104 us  [spread(): return lax.psum(jnp.where(mine, x, jnp.zeros_like(x)), axis)]
    reduce_scatter x2, waiting for transfers between devices: 40.2 us -> 53.5 us  [sweep(): lax.psum_scatter(-product(trailing, col_block), 'col', scatter_dimension=...]
  transfers between devices with their start and end apart: 6 -> 8, of which waited for: 6 -> 8; matrix products, arithmetic and copies ran while one was open for 7% -> 3% of each run, Pallas kernels for 0% -> 0%
where the time goes in v1:
time: 627 us
  waiting for transfers between devices  538 us (86%)
  matrix products  62.8 us (10%)
  between operations  14.3 us (2%)
  other arithmetic  9.5 us (2%)
    psum x1, waiting for transfers between devices, body(): lax.psum((product(column_one.T, normal_two), product(normal_two.T, local_...  149 us
    psum x1, waiting for transfers between devices, body(): diag_total = lax.psum(half, 'row')  118 us
    psum x1, waiting for transfers between devices, spread(): return lax.psum(jnp.where(mine, x, jnp.zeros_like(x)), axis)  104 us
    dot_general x14, matrix products, product(): jnp.dot(left, right, precision=lax.Precision.HIGHEST, preferred_element_t...  62.8 us
    psum x1, waiting for transfers between devices, body(): half = lax.psum(quad_one, 'col')  58.8 us
    all_gather x2, waiting for transfers between devices, panel_apart(): row_block = lax.all_gather(normal, 'col', axis=0, tiled=True)  55.2 us
    reduce_scatter x2, waiting for transfers between devices, sweep(): lax.psum_scatter(-product(trailing, col_block), 'col', scatter_dimension=...  53.5 us
  transfers between devices with their start and end apart: 8, of which 8 were waited for; matrix products, arithmetic and copies ran while one was open for 3% of the time, Pallas kernels for 0%

profile of v1, /device:TPU:1, one launch (start us, length us, event | category | flops | bytes accessed | tf_op | source)
XLA Modules:
  0.0 627.1 jit_solution(274406606482709743)
XLA Ops:
  8.1 2.7 convolution_multiply_fusion.1
  10.9 28.8 %all-gather.3.cloned.1.call-done = f32[1024,512]{1,0:T(8,128)} async-done(((f32[128,512]{1,0:T(8,128)}), f32[1024,512]{1,0:T(8,128)}) %all-gather.3.cloned.1.call-update) | async-done | bytes 2097168 | tf_op jit(solution)/shard_map/all_gather | solution.py:25
  39.8 4.2 broadcast_select_fusion.3
  44.1 103.6 %all-reduce.14.cloned.1.call-done = (f32[1024,512]{1,0:T(8,128)}, f32[1024,512]{1,0:T(8,128)}) async-done(((f32[1024,512]{1,0:T(8,128)}, f32[1024,512]{1,0:T(8,128)}), (f32[1024,512]{1,0:T(8,128)}, f32[1024,512]{1,0:T(8,128)})) %all-reduce.14.cloned.1.call-update) | async-done | bytes 4194320 | tf_op jit(solution)/shard_map/psum | solution.py:11
  147.7 17.6 %negate_bitcast_fusion.1 = f32[1024,512]{1,0:T(8,128)} fusion(f32[1024,2048]{1,0:T(8,128)} %param.8, f32[1024,512]{1,0:T(8,128)} %get-tuple-element.10, f32[1024,512]{1,0:T(8,128)} %get-tuple-element.11), kind=kOutput, calls=%fused_computation.9 | convolution fusion | flops 12886474752 | bytes 14680064 | tf_op jit(solution)/shard_map/dot_general | solution.py:15
  166.3 1.4 convolution_multiply_fusion
  167.8 28.3 %reduce-scatter.3.cloned.1.call-done = f32[128,512]{1,0:T(8,128)} async-done(((f32[1024,512]{1,0:T(8,128)}), f32[128,512]{1,0:T(8,128)}) %reduce-scatter.3.cloned.1.call-update) | async-done | bytes 262160 | tf_op jit(solution)/shard_map/reduce_scatter | solution.py:33
  196.1 2.9 fusion.16
  199.1 26.4 %all-gather.5.cloned.1.call-done = f32[1024,512]{1,0:T(8,128)} async-done(((f32[128,512]{1,0:T(8,128)}), f32[1024,512]{1,0:T(8,128)}) %all-gather.5.cloned.1.call-update) | async-done | bytes 2097168 | tf_op jit(solution)/shard_map/all_gather | solution.py:25
  225.5 4.2 broadcast_select_fusion.1
  229.7 58.8 %all-reduce.8.cloned.1.call-done = f32[512,512]{1,0:T(8,128)} async-done(((f32[512,512]{1,0:T(8,128)}), f32[512,512]{1,0:T(8,128)}) %all-reduce.8.cloned.1.call-update) | async-done | bytes 1048592 | tf_op jit(solution)/shard_map/psum | solution.py:61
  288.6 118.3 %all-reduce.12.cloned.1.call-done = (f32[512,512]{1,0:T(8,128)}, f32[1024,512]{1,0:T(8,128)}, f32[1024,512]{1,0:T(8,128)}) async-done(((f32[512,512]{1,0:T(8,128)}, f32[1024,512]{1,0:T(8,128)}, f32[1024,512]{1,0:T(8,128)}), (f32[512,512]{1,0:T(8,128)}, f32[1024,512]{1,0:T(8,128)}, f32[1024,512]{1,0:T(8,128)})) %all-reduce.12.cloned.1.call-update) | async-done | bytes 5242896 | tf_op jit(solution)/shard_map/psum | solution.py:62
  406.9 17.6 %negate_bitcast_fusion = f32[1024,512]{1,0:T(8,128)} fusion(f32[1024,2048]{1,0:T(8,128)} %param.8, f32[1024,512]{1,0:T(8,128)} %get-tuple-element.8, f32[1024,512]{1,0:T(8,128)} %get-tuple-element.9), kind=kOutput, calls=%fused_computation.8 | convolution fusion | flops 12886474752 | bytes 14680064 | tf_op jit(solution)/shard_map/dot_general | solution.py:15
  425.7 1.8 fusion.17
  427.7 2.0 fusion.18
  429.7 25.3 %reduce-scatter.5.cloned.1.call-done = f32[128,512]{1,0:T(8,128)} async-done(((f32[1024,512]{1,0:T(8,128)}), f32[128,512]{1,0:T(8,128)}) %reduce-scatter.5.cloned.1.call-update) | async-done | bytes 262160 | tf_op jit(solution)/shard_map/reduce_scatter | solution.py:33
  455.0 2.4 add_multiply_fusion
  457.4 1.0 fusion.20
  458.5 2.0 convolution_add_fusion.1
  460.5 1.9 fusion.19
  462.4 2.8 convolution_subtract_fusion.1
  465.2 148.5 %all-reduce.10.cloned.1.call-done = (f32[512,512]{1,0:T(8,128)}, f32[512,512]{1,0:T(8,128)}) async-done(((f32[512,512]{1,0:T(8,128)}, f32[512,512]{1,0:T(8,128)}), (f32[512,512]{1,0:T(8,128)}, f32[512,512]{1,0:T(8,128)})) %all-reduce.10.cloned.1.call-update) | async-done | bytes 2097168 | tf_op jit(solution)/shard_map/psum | solution.py:68
  613.8 3.5 fusion.13
  617.3 2.9 fusion.12
  (48 shorter events, 3.4 us)
Async XLA Ops:
  7.2 158.9 %copy-start = (f32[512,512]{1,0:T(8,128)S(1)}, f32[512,512]{1,0:T(8,128)}, u32[]{:S(2)}) copy-start(f32[512,512]{1,0:T(8,128)} %param.13) | copy-start | bytes 3145732
  7.2 32.6 %all-gather.3.cloned.1.call-start = ((), (), s32[]{:S(2)}) async-start(), calls=%async_computation.2 | async-start | bytes 2359296 | tf_op jit(solution)/shard_map/all_gather | solution.py:25
  10.8 136.8 %all-reduce.14.cloned.1.call-start = ((), (), s32[]{:S(2)}) async-start(), calls=%async_computation.9 | async-start | bytes 8388608 | tf_op jit(solution)/shard_map/psum | solution.py:11
  44.0 152.1 %reduce-scatter.3.cloned.1.call-start = ((), (), s32[]{:S(2)}) async-start(), calls=%async_computation.3 | async-start | bytes 2359296 | tf_op jit(solution)/shard_map/reduce_scatter | solution.py:33
  165.3 0.7 copy-start.12
  165.3 1.0 copy-start.11
  165.3 30.8 %copy-start.5 = (f32[128,512]{1,0:T(8,128)S(1)}, f32[128,512]{1,0:T(8,128)}, u32[]{:S(2)}) copy-start(f32[128,512]{1,0:T(8,128)} %convolution_multiply_fusion.1) | copy-start | bytes 786436
  165.3 60.1 %all-gather.5.cloned.1.call-start = ((), (), s32[]{:S(2)}) async-start(), calls=%async_computation.5 | async-start | bytes 2359296 | tf_op jit(solution)/shard_map/all_gather | solution.py:25
  167.7 120.8 %all-reduce.8.cloned.1.call-start = ((), (), s32[]{:S(2)}) async-start(), calls=%async_computation.4 | async-start | bytes 2097152 | tf_op jit(solution)/shard_map/psum | solution.py:61
  199.0 207.8 %all-reduce.12.cloned.1.call-start = ((), (), s32[]{:S(2)}) async-start(), calls=%async_computation.8 | async-start | bytes 10485760 | tf_op jit(solution)/shard_map/psum | solution.py:62
  288.5 166.4 %reduce-scatter.5.cloned.1.call-start = ((), (), s32[]{:S(2)}) async-start(), calls=%async_computation.6 | async-start | bytes 2359296 | tf_op jit(solution)/shard_map/reduce_scatter | solution.py:33
  424.5 1.2 copy-start.6
  424.5 3.2 copy-start.2
  424.5 189.2 %all-reduce.10.cloned.1.call-start = ((), (), s32[]{:S(2)}) async-start(), calls=%async_computation.7 | async-start | bytes 4194304 | tf_op jit(solution)/shard_map/psum | solution.py:68
  425.7 1.9 copy-start.9
  427.7 30.7 %copy-start.4 = (f32[128,512]{1,0:T(8,128)}, f32[128,512]{1,0:T(8,128)S(1)}, u32[]{:S(2)}) copy-start(f32[128,512]{1,0:T(8,128)S(1)} %broadcast_multiply_fusion) | copy-start | bytes 786436
  455.0 3.5 copy-start.8
  460.5 1.9 copy-start.1
  460.5 1.9 copy-start.10
  613.8 3.6 copy-start.7
  617.3 3.0 copy-start.3
Sparse Core Ops, SparseCore 0:
  11.0 28.7 all-gather.2
  44.1 103.4 all-reduce.13
  165.5 30.5 reduce-scatter.2
  198.2 27.2 all-gather.4
  228.2 60.2 all-reduce.7
  292.1 114.7 all-reduce.11
  424.6 30.2 reduce-scatter.4
  461.4 152.3 all-reduce.9
